TPU v7x, 128 devices: a whole 4x4x4 slice. The times are simulated.
128 devices in a mesh: tm: 16 (over x, y), tile: 8 (over z, core).
Axes of the slice: x: 4, y: 4, z: 4, core: 2. Of those that a mesh axis runs over, the one named last changes fastest.
Arguments:
- latent: bfloat16 [32, 32, 128, 16], P('tm', 'tile'), may hold values from -6 to 6
- cache_lat: bfloat16 [2, 32, 128, 16], P(None, 'tile'), may hold values from -6 to 6
- cache_one: bfloat16 [2, 32, 128, 384], P(None, 'tile'), may hold values from -6 to 6
- cache_two: bfloat16 [2, 32, 128, 384], P(None, 'tile'), may hold values from -6 to 6
- w_in: bfloat16 [3, 3, 3, 16, 384], replicated, may hold values from -0.3125 to 0.3125
- b_in: float32 [384], replicated, may hold values from -3 to 3
- gain_one: float32 [384], replicated, may hold values from 0.1 to 1.9
- w_one: bfloat16 [3, 3, 3, 384, 384], replicated, may hold values from -0.0625 to 0.0625
- b_one: float32 [384], replicated, may hold values from -3 to 3
- gain_two: float32 [384], replicated, may hold values from 0.1 to 1.9
- w_two: bfloat16 [3, 3, 3, 384, 384], replicated, may hold values from -0.0625 to 0.0625
- b_two: float32 [384], replicated, may hold values from -3 to 3
Outputs:
- decoded: bfloat16 [32, 32, 128, 384], P('tm', 'tile')
All inputs are finite; a program needn't handle non-finite values.
Results may differ from a plain program's by a relative error of at most 0.0051.
Values may be sent and summed in bfloat16 or wider, within the bound.
A program may use at most 320 MiB of HBM per device.

v0:
```python
import jax
import jax.numpy as jnp
from jax import lax
from jax.sharding import PartitionSpec as P


def from_behind(x, axis, by):
    peers = lax.axis_size(axis)
    pairs = [(i, i + by) for i in range(peers) if 0 <= i + by < peers]
    return lax.ppermute(x, axis, pairs)


def padded_2(cells, sides, width):
    for axis, dim in sides:
        count = lax.axis_size(axis)
        ends = count - 1
        head = lax.slice_in_dim(cells, 0, width, axis=dim)
        tail = lax.slice_in_dim(cells, cells.shape[dim] - width, cells.shape[dim], axis=dim)
        cells = jnp.concatenate(
            [
                lax.ppermute(tail, axis, [(i, (i + 1) % count) for i in range(ends)]),
                cells,
                lax.ppermute(head, axis, [((i + 1) % count, i) for i in range(ends)]),
            ],
            axis=dim,
        )
    return cells


def framed(values, cache):
    starting = lax.axis_index("tm") == 0
    earlier = from_behind(values, "tm", 1)
    earlier = jnp.where(starting, cache, earlier)
    extended = jnp.concatenate([earlier, values], 0)
    extended = padded_2(extended, (("tile", 1),), 1)
    return extended


def conv_local(extended, kernel, bias):
    padded = jnp.pad(extended, ((0, 0), (0, 0), (1, 1), (0, 0)))
    frames = padded.shape[0] - 2
    height = padded.shape[1] - 2
    width = padded.shape[2] - 2
    chan = padded.shape[3]
    outc = kernel.shape[-1]
    if chan < 128:
        windows = []
        for dt in range(3):
            for dy in range(3):
                for dx in range(3):
                    windows.append(padded[dt : dt + frames, dy : dy + height, dx : dx + width])
        stacked = jnp.concatenate(windows, -1).reshape(-1, 27 * chan)
        total = jnp.dot(
            stacked, kernel.reshape(27 * chan, outc), preferred_element_type=jnp.float32
        )
        return total.reshape(frames, height, width, outc) + bias
    total = jnp.zeros((frames * height * width, outc), jnp.float32)
    for dt in range(3):
        windows = []
        for dy in range(3):
            for dx in range(3):
                windows.append(padded[dt : dt + frames, dy : dy + height, dx : dx + width])
        stacked = jnp.concatenate(windows, -1).reshape(-1, 9 * chan)
        total = total + jnp.dot(
            stacked, kernel[dt].reshape(9 * chan, outc), preferred_element_type=jnp.float32
        )
    return total.reshape(frames, height, width, outc) + bias


def rms_norm(values, gain):
    return values * lax.rsqrt(jnp.mean(values * values, -1, keepdims=True) + 1e-06) * gain


def on_device(
    latent,
    cache_lat,
    cache_one,
    cache_two,
    w_in,
    b_in,
    gain_one,
    w_one,
    b_one,
    gain_two,
    w_two,
    b_two,
):
    first = conv_local(framed(latent, cache_lat), w_in, b_in).astype(jnp.bfloat16)
    normed = jax.nn.silu(rms_norm(first.astype(jnp.float32), gain_one)).astype(jnp.bfloat16)
    middle = conv_local(framed(normed, cache_one), w_one, b_one)
    normed_two = jax.nn.silu(rms_norm(middle, gain_two)).astype(jnp.bfloat16)
    last = conv_local(framed(normed_two, cache_two), w_two, b_two)
    return (first.astype(jnp.float32) + last).astype(jnp.bfloat16)


def solution(mesh):
    return jax.shard_map(
        on_device,
        mesh=mesh,
        in_specs=(
            P("tm", "tile", None, None),
            P(None, "tile", None, None),
            P(None, "tile", None, None),
            P(None, "tile", None, None),
            P(),
            P(),
            P(),
            P(),
            P(),
            P(),
            P(),
            P(),
        ),
        out_specs=P("tm", "tile", None, None),
        check_vma=False,
    )
```

profile of v0, /device:TPU:35, one launch (start us, length us, event | category | flops | bytes accessed | tf_op | source)
XLA Modules:
  0.0 147.1 jit_solution(2484425796342627473)
XLA Ops:
  0.0 3.3 %collective-permute-start = (bf16[2,4,128,16]{2,3,1,0:T(8,128)(2,1)}, bf16[2,4,128,16]{2,3,1,0:T(8,128)(2,1)S(1)}, u32[]{:S(2)}, u32[]{:S(2)}) collective-permute-start(bf16[2,4,128,16]{2,3,1,0:T(8,128)(2,1)} %param.12), channel_id=1, source_target_pairs={{0,8},{8,16},{16,24},{24,32},{32,40},{40,48},{48,56},{56,64},{64,7... | collective-permute-start | bytes 98312 | tf_op jit(solution)/shard_map/ppermute | solution.py:10
  3.4 3.8 %collective-permute-done = bf16[2,4,128,16]{2,3,1,0:T(8,128)(2,1)S(1)} collective-permute-done((bf16[2,4,128,16]{2,3,1,0:T(8,128)(2,1)}, bf16[2,4,128,16]{2,3,1,0:T(8,128)(2,1)S(1)}, u32[]{:S(2)}, u32[]{:S(2)}) %collective-permute-start) | collective-permute-done | bytes 32800 | tf_op jit(solution)/shard_map/ppermute | solution.py:10
  7.8 5.2 %collective-permute-start.1 = (bf16[4,1,128,16]{2,3,1,0:T(8,128)(2,1)S(1)}, bf16[4,1,128,16]{2,3,1,0:T(8,128)(2,1)S(1)}, u32[]{:S(2)}, u32[]{:S(2)}) collective-permute-start(bf16[4,1,128,16]{2,3,1,0:T(8,128)(2,1)S(1)} %get-tuple-element.75), channel_id=1, source_target_pairs={{0,1},{1,2},{2,3},{3,4},{4,5},{5,6},{6,7},{8,9},{9,10},{10,11},{11... | collective-permute-start | bytes 49160 | tf_op jit(solution)/shard_map/ppermute | solution.py:21
  13.1 1.9 %collective-permute-start.2 = (bf16[4,1,128,16]{2,3,1,0:T(8,128)(2,1)S(1)}, bf16[4,1,128,16]{2,3,1,0:T(8,128)(2,1)S(1)}, u32[]{:S(2)}, u32[]{:S(2)}) collective-permute-start(bf16[4,1,128,16]{2,3,1,0:T(8,128)(2,1)S(1)} %get-tuple-element.76), channel_id=1, source_target_pairs={{1,0},{2,1},{3,2},{4,3},{5,4},{6,5},{7,6},{9,8},{10,9},{11,10},{12... | collective-permute-start | bytes 49160 | tf_op jit(solution)/shard_map/ppermute | solution.py:23
  15.0 3.1 %collective-permute-done.2 = bf16[4,1,128,16]{2,3,1,0:T(8,128)(2,1)S(1)} collective-permute-done((bf16[4,1,128,16]{2,3,1,0:T(8,128)(2,1)S(1)}, bf16[4,1,128,16]{2,3,1,0:T(8,128)(2,1)S(1)}, u32[]{:S(2)}, u32[]{:S(2)}) %collective-permute-start.2) | collective-permute-done | bytes 16416 | tf_op jit(solution)/shard_map/ppermute | solution.py:23
  22.5 1.5 %fusion.11 = (f32[2,4,128]{2,1,0:T(4,128)S(1)}, bf16[2,4,128,384]{3,2,1,0:T(8,128)(2,1)S(1)}) fusion(f32[384]{0:T(512)} %param.17, bf16[2,4,128,432]{2,3,1,0:T(8,128)(2,1)S(1)} %constant_dynamic-update-slice_fusion, bf16[432,384,1,1]{1,0,3,2:T(8,128)(2,1)S(1)} %bitcast.34), kind=kOutput, calls=%fused_computation.22 | convolution fusion | flops 341703680 | bytes 2008576 | tf_op jit(solution)/shard_map/dot_general | solution.py:53
  25.3 1.9 %collective-permute-start.3 = (bf16[2,4,128,384]{3,2,1,0:T(8,128)(2,1)S(1)}, bf16[2,4,128,384]{3,2,1,0:T(8,128)(2,1)S(1)}, u32[]{:S(2)}, u32[]{:S(2)}) collective-permute-start(bf16[2,4,128,384]{3,2,1,0:T(8,128)(2,1)S(1)} %fusion.18), channel_id=1, source_target_pairs={{0,8},{8,16},{16,24},{24,32},{32,40},{40,48},{48,56},{56,64},{64,7... | collective-permute-start | bytes 2359304 | tf_op jit(solution)/shard_map/ppermute | solution.py:10
  27.2 20.3 %collective-permute-done.3 = bf16[2,4,128,384]{3,2,1,0:T(8,128)(2,1)S(1)} collective-permute-done((bf16[2,4,128,384]{3,2,1,0:T(8,128)(2,1)S(1)}, bf16[2,4,128,384]{3,2,1,0:T(8,128)(2,1)S(1)}, u32[]{:S(2)}, u32[]{:S(2)}) %collective-permute-start.3) | collective-permute-done | bytes 786464 | tf_op jit(solution)/shard_map/ppermute | solution.py:10
  47.7 3.4 %collective-permute-start.4 = (bf16[4,1,128,384]{3,2,1,0:T(8,128)(2,1)S(1)}, bf16[4,1,128,384]{3,2,1,0:T(8,128)(2,1)S(1)}, u32[]{:S(2)}, u32[]{:S(2)}) collective-permute-start(bf16[4,1,128,384]{3,2,1,0:T(8,128)(2,1)S(1)} %get-tuple-element.65), channel_id=1, source_target_pairs={{0,1},{1,2},{2,3},{3,4},{4,5},{5,6},{6,7},{8,9},{9,10},{10,11},{11... | collective-permute-start | bytes 1179656 | tf_op jit(solution)/shard_map/ppermute | solution.py:21
  51.1 1.9 %collective-permute-start.5 = (bf16[4,1,128,384]{3,2,1,0:T(8,128)(2,1)S(1)}, bf16[4,1,128,384]{3,2,1,0:T(8,128)(2,1)S(1)}, u32[]{:S(2)}, u32[]{:S(2)}) collective-permute-start(bf16[4,1,128,384]{3,2,1,0:T(8,128)(2,1)S(1)} %get-tuple-element.66), channel_id=1, source_target_pairs={{1,0},{2,1},{3,2},{4,3},{5,4},{6,5},{7,6},{9,8},{10,9},{11,10},{12... | collective-permute-start | bytes 1179656 | tf_op jit(solution)/shard_map/ppermute | solution.py:23
  53.0 1.4 fusion.27
  54.4 1.4 collective-permute-done.4
  55.8 4.4 %collective-permute-done.5 = bf16[4,1,128,384]{3,2,1,0:T(8,128)(2,1)S(1)} collective-permute-done((bf16[4,1,128,384]{3,2,1,0:T(8,128)(2,1)S(1)}, bf16[4,1,128,384]{3,2,1,0:T(8,128)(2,1)S(1)}, u32[]{:S(2)}, u32[]{:S(2)}) %collective-permute-start.5) | collective-permute-done | bytes 393248 | tf_op jit(solution)/shard_map/ppermute | solution.py:23
  60.2 1.7 %fusion.8 = bf16[4,6,130,384]{3,2,1,0:T(8,128)(2,1)S(1)} fusion(bf16[4,1,128,384]{3,2,1,0:T(8,128)(2,1)S(1)} %collective-permute-done.5, bf16[4,1,128,384]{3,2,1,0:T(8,128)(2,1)S(1)} %collective-permute-done.4, bf16[2,4,128,384]{3,2,1,0:T(8,128)(2,1)S(1)} %fusion.18, bf16[2,4,128,384]{3,2,1,0:T(8,128)(2,1)S(1)} %broadcast_select_fusion.1), kind=kLoop, calls=%fused_computation.12 | loop fusion | flops 17971200 | bytes 4755456 | tf_op jit(solution)/shard_map/concatenate | solution.py:19
  68.8 3.9 %fusion.28 = f32[1024,384]{1,0:T(8,128)S(1)} fusion(bf16[1024,3456]{1,0:T(8,128)(2,1)S(1)} %bitcast.47, bf16[3456,384]{1,0:T(8,128)(2,1)S(1)} %bitcast.41), kind=kOutput, calls=%fused_computation.143 | convolution fusion | flops 2717908992 | bytes 11304960 | tf_op jit(solution)/shard_map/dot_general | solution.py:64
  72.7 3.9 %fusion.29 = f32[1024,384]{1,0:T(8,128)S(1)} fusion(bf16[1024,3456]{1,0:T(8,128)(2,1)S(1)} %bitcast.46, bf16[3456,384]{1,0:T(8,128)(2,1)S(1)} %bitcast.39), kind=kOutput, calls=%fused_computation.144 | convolution fusion | flops 2717908992 | bytes 11304960 | tf_op jit(solution)/shard_map/dot_general | solution.py:64
  76.6 4.1 %multiply_reduce_fusion = (f32[1024]{0:T(1024)S(1)}, f32[1024,384]{1,0:T(8,128)S(1)}) fusion(f32[384]{0:T(512)S(1)} %copy-done.5, bf16[1024,3456]{1,0:T(8,128)(2,1)S(1)} %bitcast.45, bf16[3456,384]{1,0:T(8,128)(2,1)S(1)} %bitcast.37, f32[1024,384]{1,0:T(8,128)S(1)} %fusion.28, f32[1024,384]{1,0:T(8,128)S(1)} %fusion.29), kind=kOutput, calls=%fused_computation.33 | convolution fusion | flops 2719874048 | bytes 14456320 | tf_op jit(solution)/shard_map/dot_general | solution.py:64
  81.3 2.1 %collective-permute-start.6 = (bf16[2,4,128,384]{3,2,1,0:T(8,128)(2,1)S(1)}, bf16[2,4,128,384]{3,2,1,0:T(8,128)(2,1)S(1)}, u32[]{:S(2)}, u32[]{:S(2)}) collective-permute-start(bf16[2,4,128,384]{3,2,1,0:T(8,128)(2,1)S(1)} %multiply_convert_fusion), channel_id=1, source_target_pairs={{0,8},{8,16},{16,24},{24,32},{32,40},{40,48},{48,56},{56,64},{64,7... | collective-permute-start | bytes 2359304 | tf_op jit(solution)/shard_map/ppermute | solution.py:10
  83.4 19.6 %collective-permute-done.6 = bf16[2,4,128,384]{3,2,1,0:T(8,128)(2,1)S(1)} collective-permute-done((bf16[2,4,128,384]{3,2,1,0:T(8,128)(2,1)S(1)}, bf16[2,4,128,384]{3,2,1,0:T(8,128)(2,1)S(1)}, u32[]{:S(2)}, u32[]{:S(2)}) %collective-permute-start.6) | collective-permute-done | bytes 786464 | tf_op jit(solution)/shard_map/ppermute | solution.py:10
  103.2 4.2 %collective-permute-start.7 = (bf16[4,1,128,384]{3,2,1,0:T(8,128)(2,1)S(1)}, bf16[4,1,128,384]{3,2,1,0:T(8,128)(2,1)S(1)}, u32[]{:S(2)}, u32[]{:S(2)}) collective-permute-start(bf16[4,1,128,384]{3,2,1,0:T(8,128)(2,1)S(1)} %get-tuple-element.61), channel_id=1, source_target_pairs={{0,1},{1,2},{2,3},{3,4},{4,5},{5,6},{6,7},{8,9},{9,10},{10,11},{11... | collective-permute-start | bytes 1179656 | tf_op jit(solution)/shard_map/ppermute | solution.py:21
  107.4 1.9 %collective-permute-start.8 = (bf16[4,1,128,384]{3,2,1,0:T(8,128)(2,1)S(1)}, bf16[4,1,128,384]{3,2,1,0:T(8,128)(2,1)S(1)}, u32[]{:S(2)}, u32[]{:S(2)}) collective-permute-start(bf16[4,1,128,384]{3,2,1,0:T(8,128)(2,1)S(1)} %get-tuple-element.62), channel_id=1, source_target_pairs={{1,0},{2,1},{3,2},{4,3},{5,4},{6,5},{7,6},{9,8},{10,9},{11,10},{12... | collective-permute-start | bytes 1179656 | tf_op jit(solution)/shard_map/ppermute | solution.py:23
  109.4 1.4 fusion.26
  112.1 4.4 %collective-permute-done.8 = bf16[4,1,128,384]{3,2,1,0:T(8,128)(2,1)S(1)} collective-permute-done((bf16[4,1,128,384]{3,2,1,0:T(8,128)(2,1)S(1)}, bf16[4,1,128,384]{3,2,1,0:T(8,128)(2,1)S(1)}, u32[]{:S(2)}, u32[]{:S(2)}) %collective-permute-start.8) | collective-permute-done | bytes 393248 | tf_op jit(solution)/shard_map/ppermute | solution.py:23
  116.5 1.7 %select_maximum_fusion = bf16[4,6,130,384]{3,2,1,0:T(8,128)(2,1)S(1)} fusion(bf16[4,1,128,384]{3,2,1,0:T(8,128)(2,1)S(1)} %collective-permute-done.8, bf16[4,1,128,384]{3,2,1,0:T(8,128)(2,1)S(1)} %collective-permute-done.7, bf16[2,4,128,384]{3,2,1,0:T(8,128)(2,1)S(1)} %multiply_convert_fusion, bf16[2,4,128,384]{3,2,1,0:T(8,128)(2,1)S(1)} %broadcast_select_fusion), kind=kLoop, calls=%fused_computation.3 | loop fusion | flops 17971200 | bytes 4755456 | tf_op jit(solution)/shard_map/concatenate | solution.py:19
  121.5 1.7 %slice_dynamic-update-slice_fusion.5 = (bf16[2,4,128,3456]{3,2,1,0:T(8,128)(2,1)S(1)}, bf16[2,4,128,3456]{3,2,1,0:T(8,128)(2,1)S(1)}, bf16[2,4,128,3456]{3,2,1,0:T(8,128)(2,1)}) fusion(bf16[2,4,128,3456]{3,2,1,0:T(8,128)(2,1)S(1)} %get-tuple-element.50, bf16[4,6,130,384]{3,2,1,0:T(8,128)(2,1)S(1)} %select_maximum_fusion, ...), kind=kLoop, calls=%fused_computation.41 | loop fusion | bytes 4718592
  124.5 1.4 constant_dynamic-update-slice_fusion.30
  125.9 1.7 %slice_dynamic-update-slice_fusion.3 = (bf16[2,4,128,3456]{3,2,1,0:T(8,128)(2,1)S(1)}, bf16[2,4,128,3456]{3,2,1,0:T(8,128)(2,1)S(1)}, bf16[2,4,128,3456]{3,2,1,0:T(8,128)(2,1)}) fusion(bf16[2,4,128,3456]{3,2,1,0:T(8,128)(2,1)S(1)} %get-tuple-element.67, bf16[4,6,130,384]{3,2,1,0:T(8,128)(2,1)S(1)} %select_maximum_fusion, ...), kind=kLoop, calls=%fused_computation.39 | loop fusion | bytes 4718592
  129.0 1.4 slice_dynamic-update-slice_fusion.1
  130.4 1.7 %slice_dynamic-update-slice_fusion = (bf16[2,4,128,3456]{3,2,1,0:T(8,128)(2,1)S(1)}, bf16[2,4,128,3456]{3,2,1,0:T(8,128)(2,1)S(1)}, bf16[2,4,128,3456]{3,2,1,0:T(8,128)(2,1)}) fusion(bf16[2,4,128,3456]{3,2,1,0:T(8,128)(2,1)S(1)} %get-tuple-element.47, bf16[4,6,130,384]{3,2,1,0:T(8,128)(2,1)S(1)} %select_maximum_fusion, ...), kind=kLoop, calls=%fused_computation.36 | loop fusion | bytes 4718592 | tf_op jit(solution)/shard_map/concatenate | solution.py:63
  132.1 6.1 %fusion.30 = f32[1024,384]{1,0:T(8,128)S(1)} fusion(bf16[1024,3456]{1,0:T(8,128)(2,1)} %bitcast.50, bf16[3456,384]{1,0:T(8,128)(2,1)S(1)} %bitcast.42), kind=kOutput, calls=%fused_computation.145 | convolution fusion | flops 2717908992 | bytes 11304960 | tf_op jit(solution)/shard_map/dot_general | solution.py:64
  138.2 3.9 %fusion.31 = f32[1024,384]{1,0:T(8,128)S(1)} fusion(bf16[1024,3456]{1,0:T(8,128)(2,1)S(1)} %bitcast.49, bf16[3456,384]{1,0:T(8,128)(2,1)S(1)} %bitcast.40), kind=kOutput, calls=%fused_computation.146 | convolution fusion | flops 2717908992 | bytes 11304960 | tf_op jit(solution)/shard_map/dot_general | solution.py:64
  142.1 3.9 %add_add_fusion = f32[1024,384]{1,0:T(8,128)S(1)} fusion(f32[1024,384]{1,0:T(8,128)S(1)} %fusion.30, f32[1024,384]{1,0:T(8,128)S(1)} %fusion.31, bf16[1024,3456]{1,0:T(8,128)(2,1)S(1)} %bitcast.48, bf16[3456,384]{1,0:T(8,128)(2,1)S(1)} %bitcast.38), kind=kOutput, calls=%fused_computation.31 | convolution fusion | flops 2718695424 | bytes 14450688 | tf_op jit(solution)/shard_map/dot_general | solution.py:64
  (78 shorter events, 22.4 us)
Async XLA Ops:
  0.0 22.5 %copy-start = (bf16[3,3,3,16,384]{4,3,2,1,0:T(8,128)(2,1)S(1)}, bf16[3,3,3,16,384]{4,3,2,1,0:T(8,128)(2,1)}, u32[]{:S(2)}) copy-start(bf16[3,3,3,16,384]{4,3,2,1,0:T(8,128)(2,1)} %param.16) | copy-start | bytes 995332
  0.0 47.5 %copy-start.3 = (bf16[2,4,128,384]{3,2,1,0:T(8,128)(2,1)S(1)}, bf16[2,4,128,384]{3,2,1,0:T(8,128)(2,1)}, u32[]{:S(2)}) copy-start(bf16[2,4,128,384]{3,2,1,0:T(8,128)(2,1)} %param.14) | copy-start | bytes 2359300
  0.0 7.1 %collective-permute-start = (bf16[2,4,128,16]{2,3,1,0:T(8,128)(2,1)}, bf16[2,4,128,16]{2,3,1,0:T(8,128)(2,1)S(1)}, u32[]{:S(2)}, u32[]{:S(2)}) collective-permute-start(bf16[2,4,128,16]{2,3,1,0:T(8,128)(2,1)} %param.12), channel_id=1, source_target_pairs={{0,8},{8,16},{16,24},{24,32},{32,40},{40,48},{48,56},{56,64},{64,7... | collective-permute-start | bytes 98312 | tf_op jit(solution)/shard_map/ppermute | solution.py:10
  3.3 49.7 %copy-start.2 = (bf16[3,3,3,384,384]{4,3,2,1,0:T(8,128)(2,1)S(1)}, bf16[3,3,3,384,384]{4,3,2,1,0:T(8,128)(2,1)}, u32[]{:S(2)}) copy-start(bf16[3,3,3,384,384]{4,3,2,1,0:T(8,128)(2,1)} %param.19) | copy-start | bytes 23887876
  7.8 7.2 %collective-permute-start.1 = (bf16[4,1,128,16]{2,3,1,0:T(8,128)(2,1)S(1)}, bf16[4,1,128,16]{2,3,1,0:T(8,128)(2,1)S(1)}, u32[]{:S(2)}, u32[]{:S(2)}) collective-permute-start(bf16[4,1,128,16]{2,3,1,0:T(8,128)(2,1)S(1)} %get-tuple-element.75), channel_id=1, source_target_pairs={{0,1},{1,2},{2,3},{3,4},{4,5},{5,6},{6,7},{8,9},{9,10},{10,11},{11... | collective-permute-start | bytes 49160 | tf_op jit(solution)/shard_map/ppermute | solution.py:21
  13.1 5.1 %collective-permute-start.2 = (bf16[4,1,128,16]{2,3,1,0:T(8,128)(2,1)S(1)}, bf16[4,1,128,16]{2,3,1,0:T(8,128)(2,1)S(1)}, u32[]{:S(2)}, u32[]{:S(2)}) collective-permute-start(bf16[4,1,128,16]{2,3,1,0:T(8,128)(2,1)S(1)} %get-tuple-element.76), channel_id=1, source_target_pairs={{1,0},{2,1},{3,2},{4,3},{5,4},{6,5},{7,6},{9,8},{10,9},{11,10},{12... | collective-permute-start | bytes 49160 | tf_op jit(solution)/shard_map/ppermute | solution.py:23
  25.3 22.2 %collective-permute-start.3 = (bf16[2,4,128,384]{3,2,1,0:T(8,128)(2,1)S(1)}, bf16[2,4,128,384]{3,2,1,0:T(8,128)(2,1)S(1)}, u32[]{:S(2)}, u32[]{:S(2)}) collective-permute-start(bf16[2,4,128,384]{3,2,1,0:T(8,128)(2,1)S(1)} %fusion.18), channel_id=1, source_target_pairs={{0,8},{8,16},{16,24},{24,32},{32,40},{40,48},{48,56},{56,64},{64,7... | collective-permute-start | bytes 2359304 | tf_op jit(solution)/shard_map/ppermute | solution.py:10
  47.7 8.1 %collective-permute-start.4 = (bf16[4,1,128,384]{3,2,1,0:T(8,128)(2,1)S(1)}, bf16[4,1,128,384]{3,2,1,0:T(8,128)(2,1)S(1)}, u32[]{:S(2)}, u32[]{:S(2)}) collective-permute-start(bf16[4,1,128,384]{3,2,1,0:T(8,128)(2,1)S(1)} %get-tuple-element.65), channel_id=1, source_target_pairs={{0,1},{1,2},{2,3},{3,4},{4,5},{5,6},{6,7},{8,9},{9,10},{10,11},{11... | collective-permute-start | bytes 1179656 | tf_op jit(solution)/shard_map/ppermute | solution.py:21
  51.1 9.1 %collective-permute-start.5 = (bf16[4,1,128,384]{3,2,1,0:T(8,128)(2,1)S(1)}, bf16[4,1,128,384]{3,2,1,0:T(8,128)(2,1)S(1)}, u32[]{:S(2)}, u32[]{:S(2)}) collective-permute-start(bf16[4,1,128,384]{3,2,1,0:T(8,128)(2,1)S(1)} %get-tuple-element.66), channel_id=1, source_target_pairs={{1,0},{2,1},{3,2},{4,3},{5,4},{6,5},{7,6},{9,8},{10,9},{11,10},{12... | collective-permute-start | bytes 1179656 | tf_op jit(solution)/shard_map/ppermute | solution.py:23
  72.7 3.9 %copy-start.5 = (f32[384]{0:T(512)S(1)}, f32[384]{0:T(512)}, u32[]{:S(2)}) copy-start(f32[384]{0:T(512)} %param.20) | copy-start | bytes 4612
  76.6 32.8 %slice-start = ((s8[7962624]{0:T(1024)(128)(4,1)}), s8[4194304]{0:T(1024)(128)(4,1)S(1)}, s32[]{:S(2)}) async-start(s8[7962624]{0:T(1024)(128)(4,1)} %bitcast.35), calls=%async_computation | async-start | bytes 8388608
  76.6 4.1 %copy-start.6 = (f32[384]{0:T(512)S(1)}, f32[384]{0:T(512)}, u32[]{:S(2)}) copy-start(f32[384]{0:T(512)} %param.21) | copy-start | bytes 4612
  76.6 26.4 %copy-start.4 = (bf16[2,4,128,384]{3,2,1,0:T(8,128)(2,1)S(1)}, bf16[2,4,128,384]{3,2,1,0:T(8,128)(2,1)}, u32[]{:S(2)}) copy-start(bf16[2,4,128,384]{3,2,1,0:T(8,128)(2,1)} %param.15) | copy-start | bytes 2359300
  76.6 32.7 %slice-start.1 = ((s8[7962624]{0:T(1024)(128)(4,1)}), s8[3768320]{0:T(1024)(128)(4,1)S(1)}, s32[]{:S(2)}) async-start(s8[7962624]{0:T(1024)(128)(4,1)} %bitcast.35), calls=%async_computation.1 | async-start | bytes 7536640
  81.3 21.8 %collective-permute-start.6 = (bf16[2,4,128,384]{3,2,1,0:T(8,128)(2,1)S(1)}, bf16[2,4,128,384]{3,2,1,0:T(8,128)(2,1)S(1)}, u32[]{:S(2)}, u32[]{:S(2)}) collective-permute-start(bf16[2,4,128,384]{3,2,1,0:T(8,128)(2,1)S(1)} %multiply_convert_fusion), channel_id=1, source_target_pairs={{0,8},{8,16},{16,24},{24,32},{32,40},{40,48},{48,56},{56,64},{64,7... | collective-permute-start | bytes 2359304 | tf_op jit(solution)/shard_map/ppermute | solution.py:10
  103.2 8.9 %collective-permute-start.7 = (bf16[4,1,128,384]{3,2,1,0:T(8,128)(2,1)S(1)}, bf16[4,1,128,384]{3,2,1,0:T(8,128)(2,1)S(1)}, u32[]{:S(2)}, u32[]{:S(2)}) collective-permute-start(bf16[4,1,128,384]{3,2,1,0:T(8,128)(2,1)S(1)} %get-tuple-element.61), channel_id=1, source_target_pairs={{0,1},{1,2},{2,3},{3,4},{4,5},{5,6},{6,7},{8,9},{9,10},{10,11},{11... | collective-permute-start | bytes 1179656 | tf_op jit(solution)/shard_map/ppermute | solution.py:21
  107.4 9.1 %collective-permute-start.8 = (bf16[4,1,128,384]{3,2,1,0:T(8,128)(2,1)S(1)}, bf16[4,1,128,384]{3,2,1,0:T(8,128)(2,1)S(1)}, u32[]{:S(2)}, u32[]{:S(2)}) collective-permute-start(bf16[4,1,128,384]{3,2,1,0:T(8,128)(2,1)S(1)} %get-tuple-element.62), channel_id=1, source_target_pairs={{1,0},{2,1},{3,2},{4,3},{5,4},{6,5},{7,6},{9,8},{10,9},{11,10},{12... | collective-permute-start | bytes 1179656 | tf_op jit(solution)/shard_map/ppermute | solution.py:23
  142.0 5.0 %copy-start.1 = (bf16[3,3,3,16,384]{4,3,2,1,0:T(8,128)(2,1)S(1)}, bf16[3,3,3,16,384]{4,3,2,1,0:T(8,128)(2,1)}, u32[]{:S(2)}) copy-start(bf16[3,3,3,16,384]{4,3,2,1,0:T(8,128)(2,1)} %param.16) | copy-start | bytes 995332
  142.1 3.9 %copy-start.7 = (f32[384]{0:T(512)S(1)}, f32[384]{0:T(512)}, u32[]{:S(2)}) copy-start(f32[384]{0:T(512)} %param.23) | copy-start | bytes 4612
where the time goes:
time: 148 us; the launch traced here: 147 us
  waiting for transfers between devices  58.3 us (39%)
  matrix products  27.1 us (18%)
  starting transfers between devices  26 us (18%)
  local copies, waits for them, and re-layouts  21.9 us (15%)
  other arithmetic  13.2 us (9%)
    ppermute x3, waiting for transfers between devices, from_behind(): return lax.ppermute(x, axis, pairs)  43.7 us
    dot_general x6, matrix products, conv_local(): jnp.dot(stacked, kernel[dt].reshape(9 * chan, outc), preferred_element_ty...  25.6 us
    unnamed x59, local copies, waits for them, and re-layouts  16.5 us
    ppermute x3, starting transfers between devices, padded_2(): lax.ppermute(tail, axis, [(i, (i + 1) % count) for i in range(ends)])  12.8 us
    ppermute x3, waiting for transfers between devices, padded_2(): lax.ppermute(head, axis, [((i + 1) % count, i) for i in range(ends)])  11.9 us
    ppermute x3, starting transfers between devices, from_behind(): return lax.ppermute(x, axis, pairs)  7.39 us
    concatenate x6, other arithmetic, padded_2(): jnp.concatenate([lax.ppermute(tail, axis, [(i, (i + 1) % count) for i in...  6.57 us
    ppermute x3, starting transfers between devices, padded_2(): lax.ppermute(head, axis, [((i + 1) % count, i) for i in range(ends)])  5.76 us
  transfers between devices with their start and end apart: 9, of which 8 were waited for; matrix products, arithmetic and copies ran while one was open for 2% of the time, Pallas kernels for 0%

commit v1 on v0

v1 whole, which is shorter than its diff:
```python
import jax
import jax.numpy as jnp
from jax import lax
from jax.experimental import pallas as pl
from jax.experimental.pallas import tpu as pltpu
from jax.sharding import PartitionSpec as P

BF = jnp.bfloat16
F32 = jnp.float32
MESH = pl.DeviceIdType.MESH
LANE = 128
C = 384
CIN = 16
CHUNK = 256
ROWS = 6
WIDE = ROWS * LANE


def silu(v):
    return v * (0.5 + 0.5 * jnp.tanh(0.5 * v))


def twice(v):
    return jnp.concatenate([v] * (CHUNK // LANE), 1)


def shift_and_add(y):
    pieces = []
    lane = lax.broadcasted_iota(jnp.int32, (C, LANE), 1)
    for b in range(y.shape[1] // LANE):
        s = slice(b * LANE, (b + 1) * LANE)
        left = jnp.where(lane == 0, 0.0, pltpu.roll(y[0:C, s], 1, 1))
        right = jnp.where(lane == LANE - 1, 0.0, pltpu.roll(y[2 * C : 3 * C, s], LANE - 1, 1))
        pieces.append(left + y[C : 2 * C, s] + right)
    return jnp.concatenate(pieces, 1)


def conv_part(source, weights, terms, start):
    x = jnp.concatenate(
        [
            source[slot, :, pl.ds(pl.multiple_of(start + dy * LANE, LANE), CHUNK)]
            for slot, _ in terms
            for dy in range(3)
        ],
        0,
    )
    w = jnp.concatenate(
        [
            jnp.concatenate([weights[dt, dy, dx] for dx in range(3)], 1)
            for _, dt in terms
            for dy in range(3)
        ],
        0,
    )
    y = lax.dot_general(w, x, (((0,), (0,)), ((), ())), preferred_element_type=F32)
    return shift_and_add(y)


def kernel(
    latent,
    cache_lat,
    cache_one,
    cache_two,
    w_in,
    b_in,
    gain_one,
    w_one,
    b_one,
    gain_two,
    w_two,
    b_two,
    out,
    lat,
    latx,
    n1,
    n2,
    h0,
    wv1,
    wv2,
    vec,
    acc,
    stage,
    cstage,
    wsem,
    csem,
    lat_s,
    lat_r,
    cs,
    cr,
    ys,
    yr,
    bs,
    br,
    rs,
    rr,
    osem,
):
    t = lax.axis_index("tm")
    z = lax.axis_index("tile")
    nt = lax.axis_size("tm")
    nz = lax.axis_size("tile")

    def dev(dt, dz):
        return (lax.rem(t + dt + nt, nt), lax.rem(z + dz + nz, nz))

    first_tile = z == 0
    last_tile = z == nz - 1

    barrier = pltpu.get_barrier_semaphore()
    senders = [(-a, b) for a in range(4) for b in (-1, 0, 1) if (a, b) != (0, 0)] + [(1, 0)]
    for a, b in senders:
        pl.semaphore_signal(barrier, inc=1, device_id=dev(a, b), device_id_type=MESH)

    w_copies = []
    for i, (src, dst) in enumerate(((w_one, wv1), (w_two, wv2))):
        for dt in range(3):
            w_copies.append(
                pltpu.make_async_copy(src.at[dt], dst.at[dt], wsem.at[3 * i + dt])
            )
    c_copies = [
        pltpu.make_async_copy(src, cstage.at[i, :, 1:5], csem.at[i])
        for i, src in enumerate((cache_one, cache_two))
    ]

    @pl.when(t <= 1)
    def _():
        c_copies[0].start()

    @pl.when(t == 0)
    def _():
        c_copies[1].start()

    for c in w_copies:
        c.start()

    eye = (
        lax.broadcasted_iota(jnp.int32, (CIN, CIN), 0)
        == lax.broadcasted_iota(jnp.int32, (CIN, CIN), 1)
    ).astype(BF)
    for src, slot in ((latent, 5), (cache_lat, 7)):
        for f in range(2):
            for r in range(4):
                lat[slot + f, 2 + r] = lax.dot_general(
                    eye, src[f, r], (((1,), (1,)), ((), ())), preferred_element_type=F32
                ).astype(BF)

    for i, ref in enumerate((b_in, gain_one, b_one, gain_two, b_two)):
        vec[i] = jnp.transpose(jnp.broadcast_to(ref[...], (LANE, C)))

    pl.semaphore_wait(barrier, len(senders))

    lat_copies = []
    for a, b in [(3, 0), (3, 1), (3, -1), (2, 0), (2, 1), (2, -1), (1, 0), (1, 1), (1, -1), (0, 1), (0, -1)]:
        i = len(lat_copies)
        k0, k1 = (6, 7) if a == 3 else ((5, 9) if a == 0 else (5, 7))
        r0, r1 = {0: (2, 6), 1: (4, 6), -1: (2, 4)}[b]
        lat_copies.append(
            pltpu.make_async_remote_copy(
                src_ref=lat.at[k0:k1, r0:r1],
                dst_ref=lat.at[k0 - 2 * a : k1 - 2 * a, r0 - 4 * b : r1 - 4 * b],
                send_sem=lat_s.at[i],
                recv_sem=lat_r.at[i],
                device_id=dev(a, b),
                device_id_type=MESH,
            )
        )
    for c in lat_copies:
        c.start()

    cache_sends = []
    for i, src in enumerate((cache_one, cache_two)):
        for j, (own, there, dz) in enumerate(((3, 0, 1), (0, 5, -1))):
            cache_sends.append(
                pltpu.make_async_remote_copy(
                    src_ref=src.at[:, own : own + 1],
                    dst_ref=cstage.at[i, :, there : there + 1],
                    send_sem=cs.at[2 * i + j],
                    recv_sem=cr.at[2 * i + j],
                    device_id=dev(0, dz),
                    device_id_type=MESH,
                )
            )

    @pl.when(t <= 1)
    def _():
        cache_sends[0].start()
        cache_sends[1].start()

    @pl.when(t == 0)
    def _():
        cache_sends[2].start()
        cache_sends[3].start()

    def turn(which, target, rows):
        for f in range(2):
            for r in rows:
                target[4 + f, :, r * LANE : (r + 1) * LANE] = jnp.transpose(cstage[which, f, r])

    def blank(target, lo, hi, rows_low, rows_high):
        if rows_low:
            @pl.when(first_tile)
            def _():
                for s in range(lo, hi):
                    target[s, :, 0:LANE] = jnp.zeros((C, LANE), BF)

        if rows_high:
            @pl.when(last_tile)
            def _():
                for s in range(lo, hi):
                    target[s, :, WIDE - LANE : WIDE] = jnp.zeros((C, LANE), BF)

    @pl.when(t <= 1)
    def _():
        c_copies[0].wait()
        turn(0, n1, range(1, 5))

    @pl.when(t == 0)
    def _():
        c_copies[1].wait()
        turn(1, n2, range(1, 5))

    for c in lat_copies:
        c.wait_recv()

    @pl.when(first_tile)
    def _():
        lat[:, 0:2] = jnp.zeros((9, 2, CIN, LANE), BF)

    @pl.when(last_tile)
    def _():
        lat[:, 6:8] = jnp.zeros((9, 2, CIN, LANE), BF)

    def shifts(s, carry):
        v = lat[s].reshape(8 * CIN, LANE).astype(F32)
        lane = lax.broadcasted_iota(jnp.int32, (8 * CIN, LANE), 1)
        left = jnp.where(lane == 0, 0.0, pltpu.roll(v, 1, 1)).astype(BF)
        right = jnp.where(lane == LANE - 1, 0.0, pltpu.roll(v, LANE - 1, 1)).astype(BF)
        latx[s, :, 0:CIN] = left.reshape(8, CIN, LANE)
        latx[s, :, CIN : 2 * CIN] = lat[s]
        latx[s, :, 2 * CIN : 3 * CIN] = right.reshape(8, CIN, LANE)
        return carry

    lax.fori_loop(0, 9, shifts, 0)

    def project(j):
        first_frame = 2 * t - 3 + j
        slots = []
        for dt in range(3):
            before = 2 * t - 5 + j + dt
            cached = jnp.logical_and(first_frame >= 0, before < 0)
            slots.append(jnp.where(cached, 9 + before, j + dt))
        x = jnp.concatenate(
            [
                jnp.concatenate([latx[slots[dt], r + dy] for dt in range(3) for dy in range(3)], 0)
                for r in range(ROWS)
            ],
            1,
        )
        y = lax.dot_general(w_in[...], x, (((0,), (0,)), ((), ())), preferred_element_type=F32)
        y = (y + jnp.concatenate([vec[0]] * ROWS, 1)).astype(BF)
        h0[j] = y
        return y

    def first_norm(j, carry):
        v = project(j).astype(F32)
        scale = lax.rsqrt(jnp.mean(v * v, 0, keepdims=True) + 1e-06)
        v = v * scale * jnp.concatenate([vec[1]] * ROWS, 1)
        n1[j] = silu(v).astype(BF)
        return carry

    lax.fori_loop(0, 4, first_norm, 0)

    @pl.when(t <= 1)
    def _():
        for c in cache_sends[0:2]:
            c.wait_recv()
        turn(0, n1, (0, 5))

    blank(n1, 0, 6, True, True)

    for c in w_copies[0:3]:
        c.wait()

    def frame_send(f, h):
        lanes = pl.ds(pl.multiple_of(LANE + CHUNK * h, LANE), CHUNK)
        i = jnp.where(f == 0, h, 3 - h)
        return pltpu.make_async_remote_copy(
            src_ref=n2.at[1 + f, :, lanes],
            dst_ref=n2.at[3 - 3 * f, :, lanes],
            send_sem=ys.at[i],
            recv_sem=yr.at[i],
            device_id=dev(2 * f - 1, 0),
            device_id_type=MESH,
        )

    def border_send(f, h):
        i = jnp.where(f == 0, h, 3 - h)
        return pltpu.make_async_remote_copy(
            src_ref=n2.at[1 + f, :, pl.ds(pl.multiple_of(LANE + 3 * LANE * h, LANE), LANE)],
            dst_ref=n2.at[1 + f, :, pl.ds(pl.multiple_of(5 * LANE - 5 * LANE * h, LANE), LANE)],
            send_sem=bs.at[i],
            recv_sem=br.at[i],
            device_id=dev(0, 2 * h - 1),
            device_id_type=MESH,
        )

    start_a = jnp.where(t == 1, 5, 0)
    start_b = jnp.where(t == 0, 4, 1)
    next_b = jnp.where(t == 0, 5, 2)

    def first_conv(i, carry):
        f = i // 2
        h = jnp.where(f == 0, i, 3 - i)
        slots = (
            jnp.where(f == 0, start_a, start_b),
            jnp.where(f == 0, 1, next_b),
            2 + f,
        )
        c1 = conv_part(n1, wv1, [(slots[dt], dt) for dt in range(3)], h * CHUNK)
        c1 = c1 + twice(vec[2])
        scale = lax.rsqrt(jnp.mean(c1 * c1, 0, keepdims=True) + 1e-06)
        v = silu(c1 * scale * twice(vec[3])).astype(BF)
        n2[1 + f, :, pl.ds(pl.multiple_of(LANE + CHUNK * h, LANE), CHUNK)] = v
        frame_send(f, h).start()
        border_send(f, h).start()
        return carry

    lax.fori_loop(0, 4, first_conv, 0)

    project(4)

    for c in w_copies[3:6]:
        c.wait()

    @pl.when(t == 0)
    def _():
        for c in cache_sends[2:4]:
            c.wait_recv()
        turn(1, n2, (0, 5))
        blank(n2, 4, 6, True, True)

    def relay(i, slot, up):
        return pltpu.make_async_remote_copy(
            src_ref=n2.at[slot, :, 4 * LANE : 5 * LANE] if up else n2.at[slot, :, LANE : 2 * LANE],
            dst_ref=n2.at[slot, :, 0:LANE] if up else n2.at[slot, :, 5 * LANE : 6 * LANE],
            send_sem=rs.at[i],
            recv_sem=rr.at[i],
            device_id=dev(0, 1 if up else -1),
            device_id_type=MESH,
        )

    relays = [relay(0, 3, False), relay(1, 3, True), relay(2, 0, True), relay(3, 0, False)]
    slot_1 = jnp.where(t == 0, 5, 1)
    slot_0 = jnp.where(t == 0, 4, 0)

    def local_part(i, carry):
        h = i // 2
        o = i % 2

        @pl.when(i == 0)
        def _():
            border_send(0, 1).wait_recv()
            border_send(1, 1).wait_recv()
            blank(n2, 1, 3, True, False)

        @pl.when(i == 2)
        def _():
            border_send(0, 0).wait_recv()
            border_send(1, 0).wait_recv()
            blank(n2, 1, 3, False, True)
            frame_send(0, 0).wait_recv()
            frame_send(0, 1).wait_recv()
            relays[0].start()
            relays[1].start()

        @pl.when(i == 3)
        def _():
            frame_send(1, 1).wait_recv()
            relays[2].start()

        part = conv_part(n2, wv2, [(slot_1, 1 - o), (2, 2 - o)], h * CHUNK)
        acc[o, h] = part
        return carry

    lax.fori_loop(0, 4, local_part, 0)

    def out_copy(o, h):
        return pltpu.make_async_copy(
            stage.at[o, pl.ds(2 * h, 2)], out.at[o, pl.ds(2 * h, 2)], osem.at[2 * o + h]
        )

    def remote_part(i, carry):
        o = 1 - i // 2
        h = i % 2

        @pl.when(i == 0)
        def _():
            relays[1].wait_recv()
            blank(n2, 3, 4, True, False)

        @pl.when(i == 1)
        def _():
            frame_send(1, 0).wait_recv()
            relays[3].start()
            relays[0].wait_recv()
            blank(n2, 3, 4, False, True)

        @pl.when(i == 2)
        def _():
            relays[2].wait_recv()
            blank(n2, 0, 1, True, False)

        @pl.when(i == 3)
        def _():
            relays[3].wait_recv()
            blank(n2, 0, 1, False, True)

        slot = jnp.where(o == 0, slot_0, 3)
        part = conv_part(n2, wv2, [(slot, 2 * o)], h * CHUNK)
        c2 = acc[o, h] + part + twice(vec[4])
        first = h0[3 + o, :, pl.ds(pl.multiple_of(LANE + CHUNK * h, LANE), CHUNK)].astype(F32)
        done = (first + c2).astype(BF)
        for r in range(2):
            stage[o, 2 * h + r] = jnp.transpose(done[:, r * LANE : (r + 1) * LANE])
        out_copy(o, h).start()
        return carry

    lax.fori_loop(0, 4, remote_part, 0)

    for c in lat_copies:
        c.wait_send()

    @pl.when(t <= 1)
    def _():
        for c in cache_sends[0:2]:
            c.wait_send()

    @pl.when(t == 0)
    def _():
        for c in cache_sends[2:4]:
            c.wait_send()

    for f in range(2):
        for h in range(2):
            frame_send(f, h).wait_send()
            border_send(f, h).wait_send()
    for c in relays:
        c.wait_send()
    for o in range(2):
        for h in range(2):
            out_copy(o, h).wait()


def on_device(
    latent,
    cache_lat,
    cache_one,
    cache_two,
    w_in,
    b_in,
    gain_one,
    w_one,
    b_one,
    gain_two,
    w_two,
    b_two,
):
    vmem = pl.BlockSpec(memory_space=pltpu.VMEM)
    hbm = pl.BlockSpec(memory_space=pl.ANY)
    dma = pltpu.SemaphoreType.DMA
    return pl.pallas_call(
        kernel,
        name="decoder_block",
        out_shape=jax.ShapeDtypeStruct((2, 4, LANE, C), BF),
        in_specs=[vmem, vmem, hbm, hbm, vmem, vmem, vmem, hbm, vmem, vmem, hbm, vmem],
        out_specs=hbm,
        scratch_shapes=[
            pltpu.VMEM((9, 8, CIN, LANE), BF),
            pltpu.VMEM((9, 8, 3 * CIN, LANE), BF),
            pltpu.VMEM((6, C, WIDE), BF),
            pltpu.VMEM((6, C, WIDE), BF),
            pltpu.VMEM((5, C, WIDE), BF),
            pltpu.VMEM((3, 3, 3, C, C), BF),
            pltpu.VMEM((3, 3, 3, C, C), BF),
            pltpu.VMEM((5, C, LANE), F32),
            pltpu.VMEM((2, 2, C, CHUNK), F32),
            pltpu.VMEM((2, 4, LANE, C), BF),
            pltpu.VMEM((2, 2, ROWS, LANE, C), BF),
            dma((6,)),
            dma((2,)),
            dma((11,)),
            dma((11,)),
            dma((4,)),
            dma((4,)),
            dma((4,)),
            dma((4,)),
            dma((4,)),
            dma((4,)),
            dma((4,)),
            dma((4,)),
            dma((4,)),
        ],
        compiler_params=pltpu.CompilerParams(
            collective_id=0, has_side_effects=True, vmem_limit_bytes=60 << 20
        ),
    )(
        latent,
        cache_lat,
        cache_one,
        cache_two,
        w_in.reshape(27 * CIN, C),
        b_in[None],
        gain_one[None],
        w_one,
        b_one[None],
        gain_two[None],
        w_two,
        b_two[None],
    )


def solution(mesh):
    return jax.shard_map(
        on_device,
        mesh=mesh,
        in_specs=(
            P("tm", "tile", None, None),
            P(None, "tile", None, None),
            P(None, "tile", None, None),
            P(None, "tile", None, None),
            P(),
            P(),
            P(),
            P(),
            P(),
            P(),
            P(),
            P(),
        ),
        out_specs=P("tm", "tile", None, None),
        check_vma=False,
    )
```

time: 148 us -> 56.1 us (0.38)
  the two profiles are of different devices: /device:TPU:35 before, /device:TPU:1 now
where the time goes in v1:
time: 56.1 us; the launch traced here: 55.7 us
  Pallas kernels  44.1 us (79%)
  local copies, waits for them, and re-layouts  11.6 us (21%)
    pallas_call x1, Pallas kernels, on_device(): pl.pallas_call(kernel, name='decoder_block', out_shape=jax.ShapeDtypeStru...  44.1 us
    unnamed x3, local copies, waits for them, and re-layouts  5.3 us
    broadcast_in_dim x1, local copies, waits for them, and re-layouts, on_device(): gain_one[None]  1.27 us
    broadcast_in_dim x1, local copies, waits for them, and re-layouts, on_device(): b_two[None]  1.27 us
    broadcast_in_dim x1, local copies, waits for them, and re-layouts, on_device(): b_in[None]  1.27 us
    broadcast_in_dim x1, local copies, waits for them, and re-layouts, on_device(): gain_two[None]  1.26 us
    broadcast_in_dim x1, local copies, waits for them, and re-layouts, on_device(): b_one[None]  1.24 us

profile of v1, /device:TPU:1, one launch (start us, length us, event | category | flops | bytes accessed | tf_op | source)
XLA Modules:
  0.0 55.7 jit_solution(1186325572040291454)
XLA Ops:
  0.0 1.3 %broadcast_in_dim.15.b_in = f32[1,384]{1,0:T(1,128)} reshape(f32[384]{0:T(512)} %param.17) | data formatting | bytes 3072 | tf_op jit(solution)/shard_map/broadcast_in_dim | solution.py:512
  1.3 1.3 %broadcast_in_dim.16.gain_one = f32[1,384]{1,0:T(1,128)} reshape(f32[384]{0:T(512)} %param.18) | data formatting | bytes 3072 | tf_op jit(solution)/shard_map/broadcast_in_dim | solution.py:513
  2.5 1.2 %broadcast_in_dim.17.b_one = f32[1,384]{1,0:T(1,128)} reshape(f32[384]{0:T(512)} %param.20) | data formatting | bytes 3072 | tf_op jit(solution)/shard_map/broadcast_in_dim | solution.py:515
  3.8 1.3 %broadcast_in_dim.18.gain_two = f32[1,384]{1,0:T(1,128)} reshape(f32[384]{0:T(512)} %param.21) | data formatting | bytes 3072 | tf_op jit(solution)/shard_map/broadcast_in_dim | solution.py:516
  5.0 1.3 %broadcast_in_dim.19.b_two = f32[1,384]{1,0:T(1,128)} reshape(f32[384]{0:T(512)} %param.23) | data formatting | bytes 3072 | tf_op jit(solution)/shard_map/broadcast_in_dim | solution.py:518
  6.3 1.6 %copy.13.latent = bf16[2,4,128,16]{3,2,1,0:T(8,128)(2,1)} copy(bf16[2,4,128,16]{2,3,1,0:T(8,128)(2,1)} %param.12) | data formatting | bytes 65536 | tf_op args[0]
  7.9 1.6 %copy.14.cache_lat = bf16[2,4,128,16]{3,2,1,0:T(8,128)(2,1)} copy(bf16[2,4,128,16]{2,3,1,0:T(8,128)(2,1)} %param.13) | data formatting | bytes 65536 | tf_op args[1]
  9.5 44.1 %decoder_block.1 = bf16[2,4,128,384]{3,2,1,0:T(8,128)(2,1)} custom-call(bf16[2,4,128,16]{3,2,1,0:T(8,128)(2,1)} %copy.13.latent, bf16[2,4,128,16]{3,2,1,0:T(8,128)(2,1)} %copy.14.cache_lat, bf16[2,4,128,384]{3,2,1,0:T(8,128)(2,1)} %cache_one.1, bf16[2,4,128,384]{3,2,1,0:T(8,128)(2,1)} %cache_two.1, bf16[432,384]{1,0:T(8,128)(2,1)} %bitcast.1, ...), custom_call_target="tpu_custom_call" | custom-call | tf_op jit(solution)/shard_map/decoder_block/pallas_call | solution.py:471
  53.6 2.1 %copy.16 = bf16[2,4,128,384]{3,2,1,0:T(8,128)(2,1)} copy(bf16[2,4,128,384]{3,2,1,0:T(8,128)(2,1)} %decoder_block.1) | data formatting | bytes 1572864

commit v2 on v1

--- a/solution.py
+++ b/solution.py
@@ -133,19 +133,11 @@
     for c in w_copies:
         c.start()
 
-    eye = (
-        lax.broadcasted_iota(jnp.int32, (CIN, CIN), 0)
-        == lax.broadcasted_iota(jnp.int32, (CIN, CIN), 1)
-    ).astype(BF)
     for src, slot in ((latent, 5), (cache_lat, 7)):
-        for f in range(2):
-            for r in range(4):
-                lat[slot + f, 2 + r] = lax.dot_general(
-                    eye, src[f, r], (((1,), (1,)), ((), ())), preferred_element_type=F32
-                ).astype(BF)
+        lat[slot : slot + 2, 2:6] = src[...]
 
     for i, ref in enumerate((b_in, gain_one, b_one, gain_two, b_two)):
-        vec[i] = jnp.transpose(jnp.broadcast_to(ref[...], (LANE, C)))
+        vec[i] = jnp.transpose(jnp.broadcast_to(ref[...].reshape(1, C), (LANE, C)))
 
     pl.semaphore_wait(barrier, len(senders))
 
@@ -504,18 +496,18 @@
             collective_id=0, has_side_effects=True, vmem_limit_bytes=60 << 20
         ),
     )(
-        latent,
-        cache_lat,
+        jnp.swapaxes(latent, 2, 3),
+        jnp.swapaxes(cache_lat, 2, 3),
         cache_one,
         cache_two,
         w_in.reshape(27 * CIN, C),
-        b_in[None],
-        gain_one[None],
+        b_in,
+        gain_one,
         w_one,
-        b_one[None],
-        gain_two[None],
+        b_one,
+        gain_two,
         w_two,
-        b_two[None],
+        b_two,
     )
 
 

time: 56.1 us -> 46.3 us (0.83)
  local copies, waits for them, and re-layouts: 11.6 us -> 2.09 us
    broadcast_in_dim x5 -> x0, local copies, waits for them, and re-layouts: 6.31 us -> none  [the longest x1 1.27 us: on_device(): gain_one[None]]
    unnamed x3 -> x1, local copies, waits for them, and re-layouts: 5.3 us -> 2.09 us
where the time goes in v2:
time: 46.3 us; the launch traced here: 46.1 us
  Pallas kernels  44 us (95%)
  local copies, waits for them, and re-layouts  2.09 us (5%)
    pallas_call x1, Pallas kernels, on_device(): pl.pallas_call(kernel, name='decoder_block', out_shape=jax.ShapeDtypeStru...  44 us
    unnamed x1, local copies, waits for them, and re-layouts  2.09 us

profile of v2, /device:TPU:1, one launch (start us, length us, event | category | flops | bytes accessed | tf_op | source)
XLA Modules:
  0.0 46.1 jit_solution(707660141947165148)
XLA Ops:
  0.0 44.0 %decoder_block.1 = bf16[2,4,128,384]{3,2,1,0:T(8,128)(2,1)} custom-call(bf16[2,4,16,128]{3,2,1,0:T(8,128)(2,1)} %bitcast.4, bf16[2,4,16,128]{3,2,1,0:T(8,128)(2,1)} %bitcast.5, bf16[2,4,128,384]{3,2,1,0:T(8,128)(2,1)} %cache_one.1, bf16[2,4,128,384]{3,2,1,0:T(8,128)(2,1)} %cache_two.1, bf16[432,384]{1,0:T(8,128)(2,1)} %bitcast.3, f32[384]{0:T(512)} %b_in.1, ...), custom_call_target="tpu_custom_call" | custom-call | tf_op jit(solution)/shard_map/decoder_block/pallas_call | solution.py:463
  44.0 2.1 %copy.14 = bf16[2,4,128,384]{3,2,1,0:T(8,128)(2,1)} copy(bf16[2,4,128,384]{3,2,1,0:T(8,128)(2,1)} %decoder_block.1) | data formatting | bytes 1572864
